TPU v7x, 32 devices: a whole 2x2x4 slice. The times are simulated.
32 devices in a mesh: grp: 2 (over y), row: 4 (over x, core), col: 4 (over z).
Axes of the slice: x: 2, y: 2, z: 4, core: 2. Of those that a mesh axis runs over, the one named last changes fastest.
Arguments:
- dosage: float32 [16384, 2048], P(('grp', 'row'), 'col'), parts along dimension 0, as said below
- phenotypes: float32 [16384, 64], P(('grp', 'row'), 'col'), parts along dimension 0, may hold values from -6 to 6
- solution: float32 [4096, 64], P(('grp', 'col')), parts along dimension 0, may hold values from -6 to 6
- inverse_factor: float32 [4096, 2048], P(('grp', 'col'), 'row'), parts along dimension 0, as said below
Outputs:
- residual: float32 [16384, 64], P(('grp', 'row'), 'col'), parts along dimension 0
- correction: float32 [4096, 64], P(('grp', 'col')), parts along dimension 0
There are 2 independent parts, one for each index of `grp`. A program takes and returns all parts, laid end to end along the dimension named above; each array names one. Nothing has to cross between parts.
Inputs may be any that keep to these rules, and one draw needn't show every extreme that they name: `dosage`: dense real-valued entries. `inverse_factor`: upper triangular: entries below the diagonal are zero, diagonal entries positive; a given preconditioner, not derived from the slab's values.
All inputs are finite; a program needn't handle non-finite values.
Results may differ from a plain program's by a relative error of at most 0.00013.
Values sent between devices are 32-bit elements; how exact they have to be, the bound alone decides.
A program may use at most 64 MiB of HBM per device.

v0:
```python
import jax
import jax.numpy as jnp
from jax import lax
from jax.sharding import PartitionSpec as P

ITERS = 2


def transposed_product(left, right):
    return lax.dot_general(
        left,
        right,
        (((0,), (0,)), ((), ())),
        precision=lax.Precision.HIGHEST,
        preferred_element_type=jnp.float32,
    )


def plain_product(left, right):
    return jnp.dot(left, right, precision=lax.Precision.HIGHEST, preferred_element_type=jnp.float32)


def local(dosage, phenotypes, solution, inverse_factor):

    def residual_parts(field):
        fitted = plain_product(dosage, field)
        own = phenotypes - lax.psum_scatter(fitted, "col", scatter_dimension=1, tiled=True)
        return (own, own)

    field = solution
    total = jnp.zeros_like(solution)
    for step in range(ITERS):
        own, whole = residual_parts(field)
        partial_value = transposed_product(dosage, lax.all_gather(own, "col", axis=1, tiled=True))
        inner = lax.psum(transposed_product(inverse_factor, lax.psum(partial_value, "row")), "col")
        change = lax.psum(plain_product(inverse_factor, inner), "row")
        field = field + change
        total = total + change
    own, whole = residual_parts(field)
    return (own, total)


def solution(mesh):
    return jax.shard_map(
        local,
        mesh=mesh,
        in_specs=(
            P(("grp", "row"), "col"),
            P(("grp", "row"), "col"),
            P(("grp", "col"), None),
            P(("grp", "col"), "row"),
        ),
        out_specs=(P(("grp", "row"), "col"), P(("grp", "col"), None)),
        check_vma=False,
    )
```

profile of v0, /device:TPU:0, one launch (start us, length us, event | category | flops | bytes accessed | tf_op | source)
XLA Modules:
  0.0 355.0 jit_solution(17227823966330348009)
XLA Ops:
  7.2 7.2 %fusion.1 = f32[2048,64]{0,1:T(8,128)} fusion(f32[2048,512]{1,0:T(8,128)} %param.4, f32[512,64]{0,1:T(8,128)} %param.6), kind=kOutput, calls=%fused_computation.9 | convolution fusion | flops 805306368 | bytes 4849664 | tf_op jit(solution)/shard_map/dot_general | solution.py:20
  14.5 0.0 all-reduce.7.cloned.1.call-start
  14.5 24.7 %reduce-scatter.4.cloned.1.call-done = f32[2048,16]{0,1:T(8,128)} async-done(((f32[2048,64]{0,1:T(8,128)}), f32[2048,16]{0,1:T(8,128)}) %reduce-scatter.4.cloned.1.call-update) | async-done | bytes 131088 | tf_op jit(solution)/shard_map/reduce_scatter | solution.py:27
  39.2 0.9 sub.9
  40.1 15.5 %all_gather.6 = f32[2048,64]{0,1:T(8,128)S(1)} all-gather(f32[2048,16]{0,1:T(8,128)S(1)} %sub.9), channel_id=1, replica_groups=mesh['grp'=2,'row'=4,'col'=4] {'col'}, dimensions={1}, use_global_device_ids=true | all-gather | bytes 655360 | tf_op jit(solution)/shard_map/all_gather | solution.py:34
  55.6 5.5 %convolution_bitcast_fusion.3 = f32[512,64]{0,1:T(8,128)} fusion(f32[2048,64]{0,1:T(8,128)S(1)} %all_gather.6, f32[2048,512]{1,0:T(8,128)} %param.4), kind=kOutput, calls=%fused_computation.3 | convolution fusion | flops 805306368 | bytes 4849664 | tf_op jit(solution)/shard_map/dot_general | solution.py:10
  61.1 0.0 all-reduce.9.cloned.1.call-start
  61.2 30.3 %all-reduce.7.cloned.1.call-done = f32[512,64]{0,1:T(8,128)} async-done(((f32[512,64]{0,1:T(8,128)}), f32[512,64]{0,1:T(8,128)}) %all-reduce.7.cloned.1.call-update) | async-done | bytes 131088 | tf_op jit(solution)/shard_map/psum | solution.py:35
  91.5 2.3 convolution_bitcast_fusion.7
  93.8 0.0 all-reduce.11.cloned.1.call-start
  93.9 35.2 %all-reduce.9.cloned.1.call-done = f32[512,64]{0,1:T(8,128)} async-done(((f32[512,64]{0,1:T(8,128)}), f32[512,64]{0,1:T(8,128)}) %all-reduce.9.cloned.1.call-update) | async-done | bytes 131088 | tf_op jit(solution)/shard_map/psum | solution.py:35
  129.1 2.7 convolution_bitcast_fusion.6
  131.8 0.0 reduce-scatter.6.cloned.1.call-start
  131.8 31.6 %all-reduce.11.cloned.1.call-done = f32[512,64]{0,1:T(8,128)} async-done(((f32[512,64]{0,1:T(8,128)}), f32[512,64]{0,1:T(8,128)}) %all-reduce.11.cloned.1.call-update) | async-done | bytes 131088 | tf_op jit(solution)/shard_map/psum | solution.py:36
  163.4 0.9 add.27
  164.3 7.0 %convolution_bitcast_fusion.1 = f32[2048,64]{0,1:T(8,128)} fusion(f32[512,64]{0,1:T(8,128)S(1)} %add.27, f32[2048,512]{1,0:T(8,128)} %param.4), kind=kOutput, calls=%fused_computation.1 | convolution fusion | flops 805306368 | bytes 4849664 | tf_op jit(solution)/shard_map/dot_general | solution.py:20
  171.4 21.9 %reduce-scatter.6.cloned.1.call-done = f32[2048,16]{0,1:T(8,128)} async-done(((f32[2048,64]{0,1:T(8,128)}), f32[2048,16]{0,1:T(8,128)}) %reduce-scatter.6.cloned.1.call-update) | async-done | bytes 131088 | tf_op jit(solution)/shard_map/reduce_scatter | solution.py:27
  193.4 0.9 sub.10
  194.3 15.6 %all_gather.7 = f32[2048,64]{0,1:T(8,128)S(1)} all-gather(f32[2048,16]{0,1:T(8,128)S(1)} %sub.10), channel_id=1, replica_groups=mesh['grp'=2,'row'=4,'col'=4] {'col'}, dimensions={1}, use_global_device_ids=true | all-gather | bytes 655360 | tf_op jit(solution)/shard_map/all_gather | solution.py:34
  209.9 5.5 %convolution_bitcast_fusion.2 = f32[512,64]{0,1:T(8,128)} fusion(f32[2048,64]{0,1:T(8,128)S(1)} %all_gather.7, f32[2048,512]{1,0:T(8,128)} %param.4), kind=kOutput, calls=%fused_computation.2 | convolution fusion | flops 805306368 | bytes 4849664 | tf_op jit(solution)/shard_map/dot_general | solution.py:10
  215.5 0.0 all-reduce.15.cloned.1.call-start
  215.5 30.2 %all-reduce.13.cloned.1.call-done = f32[512,64]{0,1:T(8,128)} async-done(((f32[512,64]{0,1:T(8,128)}), f32[512,64]{0,1:T(8,128)}) %all-reduce.13.cloned.1.call-update) | async-done | bytes 131088 | tf_op jit(solution)/shard_map/psum | solution.py:35
  245.7 2.3 convolution_bitcast_fusion.5
  248.1 0.0 all-reduce.17.cloned.1.call-start
  248.1 35.2 %all-reduce.15.cloned.1.call-done = f32[512,64]{0,1:T(8,128)} async-done(((f32[512,64]{0,1:T(8,128)}), f32[512,64]{0,1:T(8,128)}) %all-reduce.15.cloned.1.call-update) | async-done | bytes 131088 | tf_op jit(solution)/shard_map/psum | solution.py:35
  283.3 2.7 convolution_bitcast_fusion.4
  286.0 0.0 reduce-scatter.8.cloned.1.call-start
  286.1 31.6 %all-reduce.17.cloned.1.call-done = f32[512,64]{0,1:T(8,128)} async-done(((f32[512,64]{0,1:T(8,128)}), f32[512,64]{0,1:T(8,128)}) %all-reduce.17.cloned.1.call-update) | async-done | bytes 131088 | tf_op jit(solution)/shard_map/psum | solution.py:36
  317.7 7.1 %convolution_bitcast_fusion = f32[2048,64]{0,1:T(8,128)} fusion(f32[2048,512]{1,0:T(8,128)} %param.4, f32[512,64]{0,1:T(8,128)S(1)} %add.27, f32[512,64]{0,1:T(8,128)} %all-reduce.17.cloned.1.call-done), kind=kOutput, calls=%fused_computation | convolution fusion | flops 805339136 | bytes 4980736 | tf_op jit(solution)/shard_map/dot_general | solution.py:20
  324.9 0.7 add.29
  325.6 21.3 %reduce-scatter.8.cloned.1.call-done = f32[2048,16]{0,1:T(8,128)} async-done(((f32[2048,64]{0,1:T(8,128)}), f32[2048,16]{0,1:T(8,128)}) %reduce-scatter.8.cloned.1.call-update) | async-done | bytes 131088 | tf_op jit(solution)/shard_map/reduce_scatter | solution.py:27
  346.9 1.6 sub.11
  (21 shorter events, 0.3 us)
Async XLA Ops:
  7.2 84.3 %copy-start = (f32[512,512]{1,0:T(8,128)S(1)}, f32[512,512]{1,0:T(8,128)}, u32[]{:S(2)}) copy-start(f32[512,512]{1,0:T(8,128)} %param.7) | copy-start | bytes 3145732
  7.2 32.0 %copy-start.1 = (f32[2048,16]{0,1:T(8,128)S(1)}, f32[2048,16]{0,1:T(8,128)}, u32[]{:S(2)}) copy-start(f32[2048,16]{0,1:T(8,128)} %param.5) | copy-start | bytes 393220
  7.2 32.0 %reduce-scatter.4.cloned.1.call-start = ((), (), s32[]{:S(2)}) async-start(), calls=%async_computation.3 | async-start | bytes 655360 | tf_op jit(solution)/shard_map/reduce_scatter | solution.py:27
  14.5 77.0 %all-reduce.7.cloned.1.call-start = ((), (), s32[]{:S(2)}) async-start(), calls=%async_computation.4 | async-start | bytes 262144 | tf_op jit(solution)/shard_map/psum | solution.py:35
  40.1 123.3 %copy-start.2 = (f32[512,64]{0,1:T(8,128)S(1)}, f32[512,64]{0,1:T(8,128)}, u32[]{:S(2)}) copy-start(f32[512,64]{0,1:T(8,128)} %param.6) | copy-start | bytes 393220
  61.1 67.9 %all-reduce.9.cloned.1.call-start = ((), (), s32[]{:S(2)}) async-start(), calls=%async_computation.5 | async-start | bytes 262144 | tf_op jit(solution)/shard_map/psum | solution.py:35
  93.8 69.6 %all-reduce.11.cloned.1.call-start = ((), (), s32[]{:S(2)}) async-start(), calls=%async_computation.6 | async-start | bytes 262144 | tf_op jit(solution)/shard_map/psum | solution.py:36
  131.8 61.6 %reduce-scatter.6.cloned.1.call-start = ((), (), s32[]{:S(2)}) async-start(), calls=%async_computation.7 | async-start | bytes 655360 | tf_op jit(solution)/shard_map/reduce_scatter | solution.py:27
  171.4 74.3 %all-reduce.13.cloned.1.call-start = ((), (), s32[]{:S(2)}) async-start(), calls=%async_computation.8 | async-start | bytes 262144 | tf_op jit(solution)/shard_map/psum | solution.py:35
  215.5 109.4 %copy-start.3 = (f32[512,64]{0,1:T(8,128)S(1)}, f32[512,64]{0,1:T(8,128)}, u32[]{:S(2)}) copy-start(f32[512,64]{0,1:T(8,128)} %all-reduce.11.cloned.1.call-done) | copy-start | bytes 393220
  215.5 67.8 %all-reduce.15.cloned.1.call-start = ((), (), s32[]{:S(2)}) async-start(), calls=%async_computation.9 | async-start | bytes 262144 | tf_op jit(solution)/shard_map/psum | solution.py:35
  248.1 69.6 %all-reduce.17.cloned.1.call-start = ((), (), s32[]{:S(2)}) async-start(), calls=%async_computation.10 | async-start | bytes 262144 | tf_op jit(solution)/shard_map/psum | solution.py:36
  286.0 60.8 %reduce-scatter.8.cloned.1.call-start = ((), (), s32[]{:S(2)}) async-start(), calls=%async_computation.11 | async-start | bytes 655360 | tf_op jit(solution)/shard_map/reduce_scatter | solution.py:27
  317.7 7.2 %copy-start.4 = (f32[512,64]{0,1:T(8,128)S(1)}, f32[512,64]{0,1:T(8,128)}, u32[]{:S(2)}) copy-start(f32[512,64]{0,1:T(8,128)} %all-reduce.17.cloned.1.call-done) | copy-start | bytes 393220
Sparse Core Ops, SparseCore 0:
  14.6 24.5 reduce-scatter.3
  61.3 30.1 all-reduce.6
  94.4 34.6 all-reduce.8
  131.9 31.4 all-reduce.10
  171.5 21.8 reduce-scatter.5
  215.6 30.1 all-reduce.12
  248.6 34.6 all-reduce.14
  286.2 31.4 all-reduce.16
  325.0 21.8 reduce-scatter.7
where the time goes:
time: 355 us
  waiting for transfers between devices  262 us (74%)
  matrix products  42.4 us (12%)
  blocking collectives  31.1 us (9%)
  between operations  13.9 us (4%)
  other arithmetic  5.01 us (1%)
    psum x2, waiting for transfers between devices, local(): lax.psum(transposed_product(inverse_factor, lax.psum(partial_value, 'row'...  70.4 us
    reduce_scatter x3, waiting for transfers between devices, residual_parts(): lax.psum_scatter(fitted, 'col', scatter_dimension=1, tiled=True)  67.9 us
    psum x2, waiting for transfers between devices, local(): change = lax.psum(plain_product(inverse_factor, inner), 'row')  63.2 us
    psum x2, waiting for transfers between devices, local(): lax.psum(partial_value, 'row')  60.5 us
    all_gather x2, blocking collectives, local(): lax.all_gather(own, 'col', axis=1, tiled=True)  31.1 us
    dot_general x5, matrix products, plain_product(): jnp.dot(left, right, precision=lax.Precision.HIGHEST, preferred_element_t...  26.7 us
    dot_general x4, matrix products, transposed_product(): lax.dot_general(left, right, (((0,), (0,)), ((), ())), precision=lax.Prec...  15.6 us
  transfers between devices with their start and end apart: 9, of which 9 were waited for; matrix products, arithmetic and copies ran while one was open for 0% of the time, Pallas kernels for 0%

commit v1 on v0

--- a/solution.py
+++ b/solution.py
@@ -32,7 +32,12 @@
     for step in range(ITERS):
         own, whole = residual_parts(field)
         partial_value = transposed_product(dosage, lax.all_gather(own, "col", axis=1, tiled=True))
-        inner = lax.psum(transposed_product(inverse_factor, lax.psum(partial_value, "row")), "col")
+        inner = jnp.sum(
+            lax.all_gather(
+                transposed_product(inverse_factor, lax.psum(partial_value, "row")), "col"
+            ),
+            axis=0,
+        )
         change = lax.psum(plain_product(inverse_factor, inner), "row")
         field = field + change
         total = total + change

time: 355 us -> 315 us (0.89)
  waiting for transfers between devices: 262 us -> 194 us
  blocking collectives: 31.1 us -> 60.4 us
    psum x2 -> x0, waiting for transfers between devices: 70.4 us -> none  [local(): lax.psum(transposed_product(inverse_factor, lax.psum(partial_value, 'row'...]
    all_gather x0 -> x2, blocking collectives: none -> 29.4 us  [local(): lax.all_gather(transposed_product(inverse_factor, lax.psum(partial_value,...]
  transfers between devices with their start and end apart: 9 -> 7, of which waited for: 9 -> 7; matrix products, arithmetic and copies ran while one was open for 0% -> 0% of each run, Pallas kernels for 0% -> 0%
where the time goes in v1:
time: 315 us
  waiting for transfers between devices  194 us (62%)
  blocking collectives  60.4 us (19%)
  matrix products  39.3 us (12%)
  between operations  14.2 us (5%)
  other arithmetic  5.62 us (2%)
    reduce_scatter x3, waiting for transfers between devices, residual_parts(): lax.psum_scatter(fitted, 'col', scatter_dimension=1, tiled=True)  67.9 us
    psum x2, waiting for transfers between devices, local(): change = lax.psum(plain_product(inverse_factor, inner), 'row')  65.7 us
    psum x2, waiting for transfers between devices, local(): lax.psum(partial_value, 'row')  60.5 us
    all_gather x2, blocking collectives, local(): lax.all_gather(own, 'col', axis=1, tiled=True)  31 us
    all_gather x2, blocking collectives, local(): lax.all_gather(transposed_product(inverse_factor, lax.psum(partial_value,...  29.4 us
    dot_general x5, matrix products, plain_product(): jnp.dot(left, right, precision=lax.Precision.HIGHEST, preferred_element_t...  24.9 us
    dot_general x4, matrix products, transposed_product(): lax.dot_general(left, right, (((0,), (0,)), ((), ())), precision=lax.Prec...  14.3 us
  transfers between devices with their start and end apart: 7, of which 7 were waited for; matrix products, arithmetic and copies ran while one was open for 0% of the time, Pallas kernels for 0%

profile of v1, /device:TPU:0, one launch (start us, length us, event | category | flops | bytes accessed | tf_op | source)
XLA Modules:
  0.0 314.8 jit_solution(4018952855517623273)
XLA Ops:
  7.2 7.2 %fusion.1 = f32[2048,64]{0,1:T(8,128)} fusion(f32[2048,512]{1,0:T(8,128)} %param.4, f32[512,64]{0,1:T(8,128)} %param.6), kind=kOutput, calls=%fused_computation.9 | convolution fusion | flops 805306368 | bytes 4849664 | tf_op jit(solution)/shard_map/dot_general | solution.py:20
  14.5 24.7 %reduce-scatter.4.cloned.1.call-done = f32[2048,16]{0,1:T(8,128)} async-done(((f32[2048,64]{0,1:T(8,128)}), f32[2048,16]{0,1:T(8,128)}) %reduce-scatter.4.cloned.1.call-update) | async-done | bytes 131088 | tf_op jit(solution)/shard_map/reduce_scatter | solution.py:27
  39.2 0.9 sub.9
  40.1 15.3 %all_gather.18 = f32[2048,64]{0,1:T(8,128)S(1)} all-gather(f32[2048,16]{0,1:T(8,128)S(1)} %sub.9), channel_id=1, replica_groups=mesh['grp'=2,'row'=4,'col'=4] {'col'}, dimensions={1}, use_global_device_ids=true | all-gather | bytes 655360 | tf_op jit(solution)/shard_map/all_gather | solution.py:34
  55.5 5.5 %convolution_bitcast_fusion.3 = f32[512,64]{0,1:T(8,128)} fusion(f32[2048,64]{0,1:T(8,128)S(1)} %all_gather.18, f32[2048,512]{1,0:T(8,128)} %param.4), kind=kOutput, calls=%fused_computation.3 | convolution fusion | flops 805306368 | bytes 4849664 | tf_op jit(solution)/shard_map/dot_general | solution.py:10
  61.0 0.0 all-reduce.7.cloned.1.call-start
  61.1 30.3 %all-reduce.5.cloned.1.call-done = f32[512,64]{0,1:T(8,128)} async-done(((f32[512,64]{0,1:T(8,128)}), f32[512,64]{0,1:T(8,128)}) %all-reduce.5.cloned.1.call-update) | async-done | bytes 131088 | tf_op jit(solution)/shard_map/psum | solution.py:37
  91.4 1.7 convolution_bitcast_fusion.7
  93.1 14.7 %all-gather = f32[2048,64]{0,1:T(8,128)S(1)} all-gather(f32[512,64]{0,1:T(8,128)S(1)} %convolution_bitcast_fusion.7), channel_id=2, replica_groups=mesh['grp'=2,'row'=4,'col'=4] {'col'}, dimensions={0}, use_global_device_ids=true | all-gather | bytes 655360 | tf_op jit(solution)/shard_map/all_gather | solution.py:36
  107.8 0.3 reshape.4
  108.1 0.3 reduce_sum.18
  108.4 1.8 convolution_bitcast_fusion.6
  110.2 0.0 reduce-scatter.6.cloned.1.call-start
  110.3 32.8 %all-reduce.7.cloned.1.call-done = f32[512,64]{0,1:T(8,128)} async-done(((f32[512,64]{0,1:T(8,128)}), f32[512,64]{0,1:T(8,128)}) %all-reduce.7.cloned.1.call-update) | async-done | bytes 131088 | tf_op jit(solution)/shard_map/psum | solution.py:41
  143.1 0.9 add.23
  144.1 7.0 %convolution_bitcast_fusion.1 = f32[2048,64]{0,1:T(8,128)} fusion(f32[512,64]{0,1:T(8,128)S(1)} %add.23, f32[2048,512]{1,0:T(8,128)} %param.4), kind=kOutput, calls=%fused_computation.1 | convolution fusion | flops 805306368 | bytes 4849664 | tf_op jit(solution)/shard_map/dot_general | solution.py:20
  151.1 0.0 all-reduce.9.cloned.1.call-start
  151.2 22.0 %reduce-scatter.6.cloned.1.call-done = f32[2048,16]{0,1:T(8,128)} async-done(((f32[2048,64]{0,1:T(8,128)}), f32[2048,16]{0,1:T(8,128)}) %reduce-scatter.6.cloned.1.call-update) | async-done | bytes 131088 | tf_op jit(solution)/shard_map/reduce_scatter | solution.py:27
  173.1 0.9 sub.10
  174.1 15.6 %all_gather.21 = f32[2048,64]{0,1:T(8,128)S(1)} all-gather(f32[2048,16]{0,1:T(8,128)S(1)} %sub.10), channel_id=1, replica_groups=mesh['grp'=2,'row'=4,'col'=4] {'col'}, dimensions={1}, use_global_device_ids=true | all-gather | bytes 655360 | tf_op jit(solution)/shard_map/all_gather | solution.py:34
  189.7 5.5 %convolution_bitcast_fusion.2 = f32[512,64]{0,1:T(8,128)} fusion(f32[2048,64]{0,1:T(8,128)S(1)} %all_gather.21, f32[2048,512]{1,0:T(8,128)} %param.4), kind=kOutput, calls=%fused_computation.2 | convolution fusion | flops 805306368 | bytes 4849664 | tf_op jit(solution)/shard_map/dot_general | solution.py:10
  195.3 30.2 %all-reduce.9.cloned.1.call-done = f32[512,64]{0,1:T(8,128)} async-done(((f32[512,64]{0,1:T(8,128)}), f32[512,64]{0,1:T(8,128)}) %all-reduce.9.cloned.1.call-update) | async-done | bytes 131088 | tf_op jit(solution)/shard_map/psum | solution.py:37
  225.5 1.7 convolution_bitcast_fusion.5
  227.1 14.7 %all-gather.1 = f32[2048,64]{0,1:T(8,128)S(1)} all-gather(f32[512,64]{0,1:T(8,128)S(1)} %convolution_bitcast_fusion.5), channel_id=3, replica_groups=mesh['grp'=2,'row'=4,'col'=4] {'col'}, dimensions={0}, use_global_device_ids=true | all-gather | bytes 655360 | tf_op jit(solution)/shard_map/all_gather | solution.py:36
  241.8 0.3 reshape.5
  242.2 0.3 reduce_sum.19
  242.5 1.8 convolution_bitcast_fusion.4
  244.4 32.8 %all-reduce.11.cloned.1.call-done = f32[512,64]{0,1:T(8,128)} async-done(((f32[512,64]{0,1:T(8,128)}), f32[512,64]{0,1:T(8,128)}) %all-reduce.11.cloned.1.call-update) | async-done | bytes 131088 | tf_op jit(solution)/shard_map/psum | solution.py:41
  277.2 7.1 %convolution_bitcast_fusion = f32[2048,64]{0,1:T(8,128)} fusion(f32[2048,512]{1,0:T(8,128)} %param.4, f32[512,64]{0,1:T(8,128)S(1)} %add.23, f32[512,64]{0,1:T(8,128)} %all-reduce.11.cloned.1.call-done), kind=kOutput, calls=%fused_computation | convolution fusion | flops 805339136 | bytes 4980736 | tf_op jit(solution)/shard_map/dot_general | solution.py:20
  284.4 0.7 add.25
  285.1 21.3 %reduce-scatter.8.cloned.1.call-done = f32[2048,16]{0,1:T(8,128)} async-done(((f32[2048,64]{0,1:T(8,128)}), f32[2048,16]{0,1:T(8,128)}) %reduce-scatter.8.cloned.1.call-update) | async-done | bytes 131088 | tf_op jit(solution)/shard_map/reduce_scatter | solution.py:27
  306.4 1.6 sub.11
  (21 shorter events, 0.3 us)
Async XLA Ops:
  7.2 84.2 %copy-start = (f32[512,512]{1,0:T(8,128)S(1)}, f32[512,512]{1,0:T(8,128)}, u32[]{:S(2)}) copy-start(f32[512,512]{1,0:T(8,128)} %param.7) | copy-start | bytes 3145732
  7.2 32.0 %copy-start.1 = (f32[2048,16]{0,1:T(8,128)S(1)}, f32[2048,16]{0,1:T(8,128)}, u32[]{:S(2)}) copy-start(f32[2048,16]{0,1:T(8,128)} %param.5) | copy-start | bytes 393220
  7.2 32.0 %reduce-scatter.4.cloned.1.call-start = ((), (), s32[]{:S(2)}) async-start(), calls=%async_computation.3 | async-start | bytes 655360 | tf_op jit(solution)/shard_map/reduce_scatter | solution.py:27
  14.5 76.9 %all-reduce.5.cloned.1.call-start = ((), (), s32[]{:S(2)}) async-start(), calls=%async_computation.4 | async-start | bytes 262144 | tf_op jit(solution)/shard_map/psum | solution.py:37
  55.5 87.7 %copy-start.2 = (f32[512,64]{0,1:T(8,128)S(1)}, f32[512,64]{0,1:T(8,128)}, u32[]{:S(2)}) copy-start(f32[512,64]{0,1:T(8,128)} %param.6) | copy-start | bytes 393220
  61.0 82.1 %all-reduce.7.cloned.1.call-start = ((), (), s32[]{:S(2)}) async-start(), calls=%async_computation.5 | async-start | bytes 262144 | tf_op jit(solution)/shard_map/psum | solution.py:41
  110.2 62.9 %reduce-scatter.6.cloned.1.call-start = ((), (), s32[]{:S(2)}) async-start(), calls=%async_computation.6 | async-start | bytes 655360 | tf_op jit(solution)/shard_map/reduce_scatter | solution.py:27
  151.1 74.3 %all-reduce.9.cloned.1.call-start = ((), (), s32[]{:S(2)}) async-start(), calls=%async_computation.7 | async-start | bytes 262144 | tf_op jit(solution)/shard_map/psum | solution.py:37
  195.2 82.0 %all-reduce.11.cloned.1.call-start = ((), (), s32[]{:S(2)}) async-start(), calls=%async_computation.8 | async-start | bytes 262144 | tf_op jit(solution)/shard_map/psum | solution.py:41
  241.8 42.5 %copy-start.3 = (f32[512,64]{0,1:T(8,128)S(1)}, f32[512,64]{0,1:T(8,128)}, u32[]{:S(2)}) copy-start(f32[512,64]{0,1:T(8,128)} %all-reduce.7.cloned.1.call-done) | copy-start | bytes 393220
  244.3 62.1 %reduce-scatter.8.cloned.1.call-start = ((), (), s32[]{:S(2)}) async-start(), calls=%async_computation.9 | async-start | bytes 655360 | tf_op jit(solution)/shard_map/reduce_scatter | solution.py:27
  277.2 7.2 %copy-start.4 = (f32[512,64]{0,1:T(8,128)S(1)}, f32[512,64]{0,1:T(8,128)}, u32[]{:S(2)}) copy-start(f32[512,64]{0,1:T(8,128)} %all-reduce.11.cloned.1.call-done) | copy-start | bytes 393220
Sparse Core Ops, SparseCore 0:
  14.6 24.5 reduce-scatter.3
  61.2 30.1 all-reduce.4
  110.4 32.7 all-reduce.6
  151.3 21.8 reduce-scatter.5
  195.3 30.0 all-reduce.8
  244.4 32.7 all-reduce.10
  284.5 21.8 reduce-scatter.7
